TPU v7x, 512 devices: a whole 4x4x16 slice. The times are simulated.
512 devices in a mesh: dp: 64 (over x, z), tensor: 8 (over y, core).
Axes of the slice: x: 4, y: 4, z: 16, core: 2. Of those that a mesh axis runs over, the one named last changes fastest.
Arguments:
- residual: bfloat16 [2048, 6144], P('dp', 'tensor'), may hold values from -16 to 16
- queries: bfloat16 [2048, 6144], P('dp', 'tensor'), may hold values from -4.5 to 4.5
- keys: bfloat16 [2048, 128, 1024], P('dp', None, 'tensor'), may hold values from -4.5 to 4.5
- values: bfloat16 [2048, 128, 1024], P('dp', None, 'tensor'), may hold values from -6 to 6
- lengths: int32 [2048], P('dp'), may hold values from 2 to 128
- norm_gain: bfloat16 [6144], P('tensor'), may hold values from 0.099609375 to 1.8984375
- expert_ids: int32 [2048, 2], P('dp'), may hold values from 0 to 7, all different within a row; in each aligned block of 32 rows (0 to 31, 32 to 63, ...) at most 16 rows name the same one
- expert_weights: float32 [2048, 2], P('dp'), may hold values from 0.2 to 1
- w_in: bfloat16 [6144, 65536], P('tensor', 'dp'), may hold values from -0.078125 to 0.078125
- w_out: bfloat16 [65536, 6144], P('dp', 'tensor'), may hold values from -0.0625 to 0.0625
Outputs:
- output: bfloat16 [2048, 6144], P('dp', 'tensor')
Inputs may be any that keep to these rules, and one draw needn't show every extreme that they name: `expert_ids`: each token names 2 different experts; at most 16 of the tokens of one index of dp name one expert, and in every draw some expert is named by exactly 16 of them.
All inputs are finite; a program needn't handle non-finite values.
Results may differ from a plain program's by a relative error of at most 0.008.
Values may be sent and summed in bfloat16 or wider, within the bound.
No kernel may reach another device: no remote copies, remote signals or barrier semaphores. Data moves between devices by JAX's collectives and lax.ppermute only.
A program may use at most 64 MiB of HBM per device.

v0:
```python
import jax
import jax.numpy as jnp
from jax import lax
from jax.sharding import Mesh, PartitionSpec as P

HEADS = 48
KV = 8
HEAD = 128
D = 6144
EXPERTS = 8
TOPK = 2
CACHE = 128
SRC_CAP = 16
BLOCKS = 64
CLASSES = 4
PER_CLASS = SRC_CAP // CLASSES
CAPACITY = 384
CLASS_ROWS = CAPACITY // CLASSES + BLOCKS * 6 // (4 * CLASSES)
META = 128
NORM_EPSILON = 1e-05
DP = ("x", "zh", "zq", "zn")
TENSOR = ("y", "core")


def attend(residual, queries, keys, values, lengths):
    tokens, width = residual.shape
    group_size = HEADS // KV
    query_rows = queries.reshape(tokens, group_size, HEAD)
    scores = jnp.einsum(
        "tjd,tld->tjl", query_rows, keys, preferred_element_type=jnp.float32
    ) * HEAD ** (-0.5)
    live_mask = (jnp.arange(CACHE, dtype=jnp.int32)[None, :] < lengths[:, None])[:, None, :]
    scores = jnp.where(live_mask, scores, -1e30)
    peak_score = jnp.max(scores, axis=-1, keepdims=True)
    powered = jnp.exp(scores - peak_score)
    probs = (powered / jnp.sum(powered, axis=-1, keepdims=True)).astype(jnp.bfloat16)
    attended = jnp.einsum("tjl,tld->tjd", probs, values, preferred_element_type=jnp.float32)
    return residual.astype(jnp.float32) + attended.reshape(tokens, width)


def copies_to(value, axis, peers):
    copies = jnp.broadcast_to(value, (peers, *value.shape))
    return lax.all_to_all(copies, axis, split_axis=0, concat_axis=0, tiled=True)


def summed_at_owner(pieces, axis):
    return jnp.sum(
        lax.all_to_all(pieces, axis, split_axis=0, concat_axis=0, tiled=True).astype(jnp.float32),
        axis=0,
    )


def earlier_sum(counts):
    before = jnp.arange(BLOCKS)[:, None] > jnp.arange(BLOCKS)[None, :]
    return jnp.sum(jnp.where(before, counts[None, :], 0), axis=1)


def shards(
    residual, queries, keys, values, lengths, norm_gain, expert_ids, expert_weights, w_in, w_out
):
    tokens, width = residual.shape
    block = (
        (lax.axis_index("x") * 2 + lax.axis_index("zh")) * 2 + lax.axis_index("zq")
    ) * 4 + lax.axis_index("zn")
    own_class = lax.axis_index("zn")
    summed = attend(residual, queries, keys, values, lengths)
    square_sums = lax.psum(jnp.sum(summed * summed, axis=1), TENSOR)
    normed = (
        summed
        * lax.rsqrt(square_sums[:, None] / D + NORM_EPSILON)
        * norm_gain.astype(jnp.float32)[None, :]
    ).astype(jnp.bfloat16)
    flat_ids = expert_ids.reshape(-1)
    pairs = flat_ids.shape[0]
    same = flat_ids[:, None] == flat_ids[None, :]
    earlier = jnp.arange(pairs)[:, None] > jnp.arange(pairs)[None, :]
    rank = jnp.sum((same & earlier).astype(jnp.int32), axis=1)
    slots = EXPERTS * SRC_CAP
    target = flat_ids * SRC_CAP + (rank + block) % CLASSES * PER_CLASS + rank // CLASSES
    pick_pairs = target[None, :] == jnp.arange(slots, dtype=jnp.int32)[:, None]
    pick_tokens = jnp.sum(
        pick_pairs.reshape(slots, tokens, TOPK).astype(jnp.float32), axis=2
    ).astype(jnp.bfloat16)
    counts = jnp.sum(
        (flat_ids[None, :] == jnp.arange(EXPERTS, dtype=jnp.int32)[:, None]).astype(jnp.float32),
        axis=1,
    ).astype(jnp.bfloat16)
    packed = jnp.dot(pick_tokens, normed, preferred_element_type=jnp.float32).astype(jnp.bfloat16)
    packed = packed.reshape(EXPERTS, 1, CLASSES, PER_CLASS, width)
    meta = jnp.broadcast_to(
        counts[:, None, None, None, None], (EXPERTS, 1, CLASSES, PER_CLASS, META)
    )
    outgoing = jnp.concatenate([packed, meta], axis=-1)
    outgoing = jnp.broadcast_to(outgoing, (EXPERTS, 2, CLASSES, PER_CLASS, width + META))
    received = lax.all_to_all(
        outgoing.reshape(BLOCKS, PER_CLASS, width + META),
        DP,
        split_axis=0,
        concat_axis=0,
        tiled=True,
    )
    named = received[:, 0, width].astype(jnp.int32)
    kept = jnp.clip(CAPACITY - earlier_sum(named), 0, named)
    shift = (own_class - jnp.arange(BLOCKS, dtype=jnp.int32)) % CLASSES
    in_class = (kept - shift + CLASSES - 1) // CLASSES
    first = earlier_sum(in_class)
    place = jnp.arange(PER_CLASS, dtype=jnp.int32)[None, :]
    spot = jnp.where(place < in_class[:, None], first[:, None] + place, -1).reshape(-1)
    compact = (spot[None, :] == jnp.arange(CLASS_ROWS, dtype=jnp.int32)[:, None]).astype(
        jnp.bfloat16
    )
    class_rows = jnp.dot(
        compact,
        received[:, :, :width].reshape(BLOCKS * PER_CLASS, width),
        preferred_element_type=jnp.float32,
    ).astype(jnp.bfloat16)
    rows = copies_to(class_rows, "zn", CLASSES).reshape(CLASSES * CLASS_ROWS, width)
    total = rows.shape[0]
    hidden_parts = jnp.dot(rows, w_in, preferred_element_type=jnp.float32).astype(jnp.bfloat16)
    unit = hidden_parts.shape[1] // 8
    pieces = jnp.moveaxis(hidden_parts.reshape(total, 2, 4, unit), 0, 2)
    core_sums = summed_at_owner(pieces, "core").astype(jnp.bfloat16)
    hidden = jax.nn.silu(summed_at_owner(core_sums.reshape(4, total, unit), "y")).astype(
        jnp.bfloat16
    )
    gathered = copies_to(hidden, "y", 4)
    gathered = lax.all_gather(gathered, "core", axis=0, tiled=True)
    hidden_all = jnp.moveaxis(gathered, 0, 1).reshape(total, 8 * unit)
    results = jnp.dot(hidden_all, w_out, preferred_element_type=jnp.float32).astype(jnp.bfloat16)
    class_out = summed_at_owner(results.reshape(CLASSES, CLASS_ROWS, width), "zn").astype(
        jnp.bfloat16
    )
    spread = (spot[:, None] == jnp.arange(CLASS_ROWS, dtype=jnp.int32)[None, :]).astype(
        jnp.bfloat16
    )
    returned = jnp.dot(spread, class_out, preferred_element_type=jnp.float32).astype(jnp.bfloat16)
    combined = lax.all_to_all(
        returned.reshape(BLOCKS, PER_CLASS, width), DP, split_axis=0, concat_axis=0, tiled=True
    )
    per_expert = jnp.sum(
        combined.reshape(EXPERTS, 2, SRC_CAP, width).astype(jnp.float32), axis=1
    ).reshape(slots, width)
    mix_rows = jnp.sum(
        (pick_pairs.astype(jnp.float32) * expert_weights.reshape(-1)[None, :]).reshape(
            slots, tokens, TOPK
        ),
        axis=2,
    )
    addition = jnp.einsum("st,sd->td", mix_rows, per_expert, precision=lax.Precision.HIGHEST)
    return (summed + addition).astype(jnp.bfloat16)


def solution(mesh):
    fine = Mesh(mesh.devices.reshape(4, 2, 2, 4, 4, 2), (*DP, *TENSOR))
    in_specs = (
        P(DP, TENSOR),
        P(DP, TENSOR),
        P(DP, None, TENSOR),
        P(DP, None, TENSOR),
        P(DP),
        P(TENSOR),
        P(DP, None),
        P(DP, None),
        P(TENSOR, DP),
        P(DP, TENSOR),
    )
    return jax.shard_map(
        shards, mesh=fine, in_specs=in_specs, out_specs=P(DP, TENSOR), check_vma=False
    )
```

profile of v0, /device:TPU:6, one launch (start us, length us, event | category | flops | bytes accessed | tf_op | source)
XLA Modules:
  0.0 185.7 jit_solution(11705358472968257919)
XLA Ops:
  0.0 0.0 copy-start
  0.0 0.0 copy-start.3
  0.0 0.0 copy-start.1
  0.0 0.0 copy-start.2
  0.0 0.0 copy-start.4
  0.0 0.9 copy.57
  0.9 0.1 eq.72
  1.1 0.2 convert_reduce_fusion.2
  1.2 0.1 convert_reduce_fusion.3
  1.4 0.7 iota_compare_fusion.7
  2.1 0.7 convert_element_type.90
  2.8 0.1 reduce_sum.118
  2.9 0.1 copy.58
  3.0 0.9 reshape.277
  3.8 1.9 %fusion.3 = f32[32,6,128]{2,1,0:T(8,128)S(1)} fusion(bf16[32,6,128]{2,1,0:T(8,128)(2,1)S(1)} %reshape.277, bf16[32,128,128]{2,1,0:T(8,128)(2,1)} %param.12, pred[32,128]{1,0:T(8,128)(4,1)S(1)} %iota_compare_fusion.7), kind=kOutput, calls=%fused_computation.9 | convolution fusion | flops 6340608 | bytes 1200128 | tf_op jit(solution)/shard_map/tjd,tld->tjl/dot_general | solution.py:29
  5.7 0.2 fusion.22
  5.9 0.0 copy-done.1
  5.9 0.6 fusion.7
  6.5 0.0 copy-done.2
  6.5 0.1 multiply_reduce_fusion
  6.7 14.9 %psum.7 = f32[32]{0:T(128)S(1)} all-reduce(f32[32]{0:T(128)S(1)} %multiply_reduce_fusion), channel_id=1, replica_groups=mesh['x'=4,'zh'=2,'zq'=2,'zn'=4,'y'=4,'core'=2] {'y','core'}, use_global_device_ids=true, to_apply=%region_6.7 | all-reduce | flops 32 | bytes 256 | tf_op jit(solution)/shard_map/psum | solution.py:67
  21.5 0.0 copy-done.3
  21.6 0.0 copy-done.4
  21.6 0.1 convert_reduce_fusion.1
  21.7 0.3 convolution_convert_fusion.3
  21.9 0.1 reshape.279
  22.0 0.1 broadcast_in_dim.46
  22.1 0.1 maximum_bitcast_fusion
  22.2 0.1 broadcast_in_dim.48
  22.3 45.3 %all_to_all.35 = bf16[64,4,896]{2,1,0:T(4,128)(2,1)S(1)} all-to-all(bf16[64,4,896]{2,1,0:T(4,128)(2,1)S(1)} %bitcast.41), channel_id=1, replica_groups=mesh['x'=4,'zh'=2,'zq'=2,'zn'=4,'y'=4,'core'=2] {'x','zh','zq','zn'}, dimensions={0} | all-to-all | bytes 917504 | tf_op jit(solution)/shard_map/all_to_all | solution.py:95
  67.6 0.1 slice.9
  67.8 0.1 reshape.281
  67.9 1.2 fusion.13
  69.1 0.1 select_reduce_fusion.1
  69.2 0.1 select_reduce_fusion
  69.3 0.1 add_select_fusion
  69.4 0.1 select_n.77
  69.6 0.2 convolution_convert_fusion.4
  69.8 18.4 %all_to_all.36 = bf16[4,120,768]{2,1,0:T(8,128)(2,1)S(1)} all-to-all(bf16[4,120,768]{2,1,0:T(8,128)(2,1)S(1)} %broadcast_in_dim.85), channel_id=1, replica_groups=mesh['x'=4,'zh'=2,'zq'=2,'zn'=4,'y'=4,'core'=2] {'zn'}, dimensions={0} | all-to-all | bytes 1474560 | tf_op jit(solution)/shard_map/all_to_all | solution.py:43
  88.3 0.0 copy-done
  88.3 1.9 %convolution_convert_fusion = bf16[480,1024]{1,0:T(8,128)(2,1)} fusion(bf16[480,768]{1,0:T(8,128)(2,1)S(1)} %bitcast.46, bf16[768,1024]{1,0:T(8,128)(2,1)S(1)} %copy-done), kind=kOutput, calls=%fused_computation.1 | convolution fusion | flops 755466240 | bytes 3293184 | tf_op jit(solution)/shard_map/dot_general | solution.py:119
  90.2 2.2 %reshape.283 = bf16[480,2,4,128]{3,2,1,0:T(4,128)(2,1)S(1)} reshape(bf16[480,1024]{1,0:T(8,128)(2,1)} %convolution_convert_fusion) | data formatting | bytes 1966080 | tf_op jit(solution)/shard_map/reshape | solution.py:121
  92.3 0.3 copy.83
  92.7 4.5 %all_to_all.37 = bf16[2,4,480,128]{3,1,2,0:T(4,128)(2,1)S(1)} all-to-all(bf16[2,4,480,128]{3,1,2,0:T(4,128)(2,1)S(1)} %bitcast.40), channel_id=1, replica_groups=mesh['x'=4,'zh'=2,'zq'=2,'zn'=4,'y'=4,'core'=2] {'core'}, dimensions={0} | all-to-all | bytes 1966080 | tf_op jit(solution)/shard_map/all_to_all | solution.py:48
  97.2 1.1 reduce_sum.125
  98.3 0.1 copy.65
  98.3 16.0 %all_to_all.38 = bf16[4,480,128]{2,1,0:T(8,128)(2,1)S(1)} all-to-all(bf16[4,480,128]{2,1,0:T(8,128)(2,1)S(1)} %copy.65), channel_id=1, replica_groups=mesh['x'=4,'zh'=2,'zq'=2,'zn'=4,'y'=4,'core'=2] {'y'}, dimensions={0} | all-to-all | bytes 983040 | tf_op jit(solution)/shard_map/all_to_all | solution.py:48
  114.3 0.1 convert_reduce_fusion
  114.4 0.1 multiply_convert_fusion
  114.5 0.0 copy-start.5
  114.5 0.1 broadcast_in_dim.86
  114.6 10.9 %all_to_all.39 = bf16[4,480,128]{2,1,0:T(8,128)(2,1)S(1)} all-to-all(bf16[4,480,128]{2,1,0:T(8,128)(2,1)S(1)} %broadcast_in_dim.86), channel_id=1, replica_groups=mesh['x'=4,'zh'=2,'zq'=2,'zn'=4,'y'=4,'core'=2] {'y'}, dimensions={0} | all-to-all | bytes 983040 | tf_op jit(solution)/shard_map/all_to_all | solution.py:43
  125.5 2.5 %all_gather.3 = bf16[8,480,128]{2,1,0:T(8,128)(2,1)S(1)} all-gather(bf16[4,480,128]{2,1,0:T(8,128)(2,1)S(1)} %all_to_all.39), channel_id=1, replica_groups=mesh['x'=4,'zh'=2,'zq'=2,'zn'=4,'y'=4,'core'=2] {'core'}, dimensions={0}, use_global_device_ids=true | all-gather | bytes 1474560 | tf_op jit(solution)/shard_map/all_gather | solution.py:127
  128.0 0.0 copy-done.5
  128.0 0.9 convolution_convert_fusion.1
  128.9 22.0 %all_to_all.40 = bf16[4,120,768]{2,1,0:T(8,128)(2,1)S(1)} all-to-all(bf16[4,120,768]{2,1,0:T(8,128)(2,1)S(1)} %bitcast.47), channel_id=1, replica_groups=mesh['x'=4,'zh'=2,'zq'=2,'zn'=4,'y'=4,'core'=2] {'zn'}, dimensions={0} | all-to-all | bytes 1474560 | tf_op jit(solution)/shard_map/all_to_all | solution.py:48
  150.9 0.1 reduce_sum.127
  151.0 0.3 convolution_convert_fusion.2
  151.3 0.1 reshape.286
  151.4 33.2 %all_to_all.41 = bf16[64,4,768]{2,1,0:T(4,128)(2,1)S(1)} all-to-all(bf16[64,4,768]{2,1,0:T(4,128)(2,1)S(1)} %reshape.286), channel_id=1, replica_groups=mesh['x'=4,'zh'=2,'zq'=2,'zn'=4,'y'=4,'core'=2] {'x','zh','zq','zn'}, dimensions={0} | all-to-all | bytes 786432 | tf_op jit(solution)/shard_map/all_to_all | solution.py:137
  184.7 0.1 reshape.289
  184.7 0.1 reduce_sum.128
  184.8 1.0 fusion.4
  (4 shorter events, 0.1 us)
Async XLA Ops:
  0.0 88.3 %copy-start = (bf16[768,1024]{1,0:T(8,128)(2,1)S(1)}, bf16[768,1024]{1,0:T(8,128)(2,1)}, u32[]{:S(2)}) copy-start(bf16[768,1024]{1,0:T(8,128)(2,1)} %param.18) | copy-start | bytes 4718596
  0.0 21.5 %copy-start.3 = (s32[32,2]{0,1:T(2,128)S(1)}, s32[32,2]{0,1:T(2,128)}, u32[]{:S(2)}) copy-start(s32[32,2]{0,1:T(2,128)} %param.16) | copy-start | bytes 772
  0.0 5.9 %copy-start.1 = (bf16[32,128,128]{2,1,0:T(8,128)(2,1)S(1)}, bf16[32,128,128]{2,1,0:T(8,128)(2,1)}, u32[]{:S(2)}) copy-start(bf16[32,128,128]{2,1,0:T(8,128)(2,1)} %param.13) | copy-start | bytes 3145732
  0.0 6.5 %copy-start.2 = (bf16[32,768]{1,0:T(8,128)(2,1)S(1)}, bf16[32,768]{1,0:T(8,128)(2,1)}, u32[]{:S(2)}) copy-start(bf16[32,768]{1,0:T(8,128)(2,1)} %param.10) | copy-start | bytes 147460
  0.0 21.5 %copy-start.4 = (f32[32,2]{0,1:T(2,128)S(1)}, f32[32,2]{0,1:T(2,128)}, u32[]{:S(2)}) copy-start(f32[32,2]{0,1:T(2,128)} %param.17) | copy-start | bytes 772
  114.5 13.5 %copy-start.5 = (bf16[1024,768]{1,0:T(8,128)(2,1)S(1)}, bf16[1024,768]{1,0:T(8,128)(2,1)}, u32[]{:S(2)}) copy-start(bf16[1024,768]{1,0:T(8,128)(2,1)} %param.19) | copy-start | bytes 4718596
where the time goes:
time: 186 us
  blocking collectives  168 us (90%)
  matrix products  6.99 us (4%)
  local copies, waits for them, and re-layouts  5.51 us (3%)
  other arithmetic  5.19 us (3%)
    all_to_all x1, blocking collectives, shards(): lax.all_to_all(outgoing.reshape(BLOCKS, PER_CLASS, width + META), DP, spl...  45.3 us
    all_to_all x3, blocking collectives, summed_at_owner(): lax.all_to_all(pieces, axis, split_axis=0, concat_axis=0, tiled=True)  42.6 us
    all_to_all x1, blocking collectives, shards(): lax.all_to_all(returned.reshape(BLOCKS, PER_CLASS, width), DP, split_axis...  33.2 us
    all_to_all x2, blocking collectives, copies_to(): return lax.all_to_all(copies, axis, split_axis=0, concat_axis=0, tiled=True)  29.3 us
    psum x1, blocking collectives, shards(): square_sums = lax.psum(jnp.sum(summed * summed, axis=1), TENSOR)  14.9 us

commit v1 on v0

--- a/solution.py
+++ b/solution.py
@@ -64,7 +64,7 @@
     ) * 4 + lax.axis_index("zn")
     own_class = lax.axis_index("zn")
     summed = attend(residual, queries, keys, values, lengths)
-    square_sums = lax.psum(jnp.sum(summed * summed, axis=1), TENSOR)
+    square_sums = lax.psum(lax.psum(jnp.sum(summed * summed, axis=1), "y"), "core")
     normed = (
         summed
         * lax.rsqrt(square_sums[:, None] / D + NORM_EPSILON)

time: 186 us -> 186 us (level)
    all_to_all x3, blocking collectives: 42.6 us -> 38.6 us  [summed_at_owner(): lax.all_to_all(pieces, axis, split_axis=0, concat_axis=0, tiled=True)]
    all_to_all x2, blocking collectives: 29.3 us -> 32.2 us  [copies_to(): return lax.all_to_all(copies, axis, split_axis=0, concat_axis=0, tiled=True)]
    all_to_all x1, blocking collectives: 45.3 us -> 47.9 us  [shards(): lax.all_to_all(outgoing.reshape(BLOCKS, PER_CLASS, width + META), DP, spl...]
    psum x1 -> x2, blocking collectives: 14.9 us -> 13.2 us  [the longest x1 10.7 us: shards(): lax.psum(jnp.sum(summed * summed, axis=1), 'y')]
where the time goes in v1:
time: 186 us
  blocking collectives  168 us (90%)
  matrix products  7 us (4%)
  local copies, waits for them, and re-layouts  5.51 us (3%)
  other arithmetic  5.19 us (3%)
    all_to_all x1, blocking collectives, shards(): lax.all_to_all(outgoing.reshape(BLOCKS, PER_CLASS, width + META), DP, spl...  47.9 us
    all_to_all x3, blocking collectives, summed_at_owner(): lax.all_to_all(pieces, axis, split_axis=0, concat_axis=0, tiled=True)  38.6 us
    all_to_all x1, blocking collectives, shards(): lax.all_to_all(returned.reshape(BLOCKS, PER_CLASS, width), DP, split_axis...  33.3 us
    all_to_all x2, blocking collectives, copies_to(): return lax.all_to_all(copies, axis, split_axis=0, concat_axis=0, tiled=True)  32.2 us
    psum x1, blocking collectives, shards(): lax.psum(jnp.sum(summed * summed, axis=1), 'y')  10.7 us

profile of v1, /device:TPU:6, one launch (start us, length us, event | category | flops | bytes accessed | tf_op | source)
XLA Modules:
  0.0 185.6 jit_solution(1657310430195651367)
XLA Ops:
  0.0 0.0 copy-start
  0.0 0.0 copy-start.1
  0.0 0.0 copy-start.2
  0.0 0.0 copy-start.3
  0.0 0.0 copy-start.4
  0.0 0.9 copy.57
  0.9 0.1 eq.72
  1.1 0.2 convert_reduce_fusion.2
  1.2 0.1 convert_reduce_fusion.3
  1.4 0.7 iota_compare_fusion.7
  2.1 0.7 convert_element_type.90
  2.8 0.1 reduce_sum.118
  2.9 0.1 copy.58
  3.0 0.9 reshape.277
  3.8 1.9 %fusion.3 = f32[32,6,128]{2,1,0:T(8,128)S(1)} fusion(bf16[32,6,128]{2,1,0:T(8,128)(2,1)S(1)} %reshape.277, bf16[32,128,128]{2,1,0:T(8,128)(2,1)} %param.12, pred[32,128]{1,0:T(8,128)(4,1)S(1)} %iota_compare_fusion.7), kind=kOutput, calls=%fused_computation.9 | convolution fusion | flops 6340608 | bytes 1200128 | tf_op jit(solution)/shard_map/tjd,tld->tjl/dot_general | solution.py:29
  5.7 0.2 fusion.22
  5.9 0.0 copy-done.1
  5.9 0.6 fusion.7
  6.5 0.0 copy-done.2
  6.5 0.1 multiply_reduce_fusion
  6.7 10.7 %psum.14 = f32[32]{0:T(128)S(1)} all-reduce(f32[32]{0:T(128)S(1)} %multiply_reduce_fusion), channel_id=1, replica_groups=mesh['x'=4,'zh'=2,'zq'=2,'zn'=4,'y'=4,'core'=2] {'y'}, use_global_device_ids=true, to_apply=%region_6.7 | all-reduce | flops 32 | bytes 256 | tf_op jit(solution)/shard_map/psum | solution.py:67
  17.4 2.4 %psum.15 = f32[32]{0:T(128)S(1)} all-reduce(f32[32]{0:T(128)S(1)} %psum.14), channel_id=1, replica_groups=mesh['x'=4,'zh'=2,'zq'=2,'zn'=4,'y'=4,'core'=2] {'core'}, use_global_device_ids=true, to_apply=%region_7.8 | all-reduce | flops 32 | bytes 256 | tf_op jit(solution)/shard_map/psum | solution.py:67
  19.9 0.0 copy-done.3
  19.9 0.0 copy-done.4
  19.9 0.1 convert_reduce_fusion.1
  20.0 0.3 convolution_convert_fusion.3
  20.3 0.1 reshape.279
  20.3 0.1 broadcast_in_dim.46
  20.4 0.1 maximum_bitcast_fusion
  20.5 0.1 broadcast_in_dim.48
  20.6 47.9 %all_to_all.35 = bf16[64,4,896]{2,1,0:T(4,128)(2,1)S(1)} all-to-all(bf16[64,4,896]{2,1,0:T(4,128)(2,1)S(1)} %bitcast.41), channel_id=1, replica_groups=mesh['x'=4,'zh'=2,'zq'=2,'zn'=4,'y'=4,'core'=2] {'x','zh','zq','zn'}, dimensions={0} | all-to-all | bytes 917504 | tf_op jit(solution)/shard_map/all_to_all | solution.py:95
  68.5 0.1 slice.9
  68.6 0.1 reshape.281
  68.7 1.2 fusion.13
  70.0 0.1 select_reduce_fusion.1
  70.1 0.1 select_reduce_fusion
  70.2 0.1 add_select_fusion
  70.3 0.1 select_n.77
  70.4 0.2 convolution_convert_fusion.4
  70.7 20.8 %all_to_all.36 = bf16[4,120,768]{2,1,0:T(8,128)(2,1)S(1)} all-to-all(bf16[4,120,768]{2,1,0:T(8,128)(2,1)S(1)} %broadcast_in_dim.85), channel_id=1, replica_groups=mesh['x'=4,'zh'=2,'zq'=2,'zn'=4,'y'=4,'core'=2] {'zn'}, dimensions={0} | all-to-all | bytes 1474560 | tf_op jit(solution)/shard_map/all_to_all | solution.py:43
  91.5 0.0 copy-done
  91.5 1.9 %convolution_convert_fusion = bf16[480,1024]{1,0:T(8,128)(2,1)} fusion(bf16[480,768]{1,0:T(8,128)(2,1)S(1)} %bitcast.46, bf16[768,1024]{1,0:T(8,128)(2,1)S(1)} %copy-done), kind=kOutput, calls=%fused_computation.1 | convolution fusion | flops 755466240 | bytes 3293184 | tf_op jit(solution)/shard_map/dot_general | solution.py:119
  93.4 2.2 %reshape.283 = bf16[480,2,4,128]{3,2,1,0:T(4,128)(2,1)S(1)} reshape(bf16[480,1024]{1,0:T(8,128)(2,1)} %convolution_convert_fusion) | data formatting | bytes 1966080 | tf_op jit(solution)/shard_map/reshape | solution.py:121
  95.5 0.3 copy.83
  95.9 4.5 %all_to_all.37 = bf16[2,4,480,128]{3,1,2,0:T(4,128)(2,1)S(1)} all-to-all(bf16[2,4,480,128]{3,1,2,0:T(4,128)(2,1)S(1)} %bitcast.40), channel_id=1, replica_groups=mesh['x'=4,'zh'=2,'zq'=2,'zn'=4,'y'=4,'core'=2] {'core'}, dimensions={0} | all-to-all | bytes 1966080 | tf_op jit(solution)/shard_map/all_to_all | solution.py:48
  100.4 1.1 reduce_sum.125
  101.4 0.1 copy.65
  101.5 12.1 %all_to_all.38 = bf16[4,480,128]{2,1,0:T(8,128)(2,1)S(1)} all-to-all(bf16[4,480,128]{2,1,0:T(8,128)(2,1)S(1)} %copy.65), channel_id=1, replica_groups=mesh['x'=4,'zh'=2,'zq'=2,'zn'=4,'y'=4,'core'=2] {'y'}, dimensions={0} | all-to-all | bytes 983040 | tf_op jit(solution)/shard_map/all_to_all | solution.py:48
  113.6 0.1 convert_reduce_fusion
  113.7 0.1 multiply_convert_fusion
  113.8 0.0 copy-start.5
  113.8 0.1 broadcast_in_dim.86
  113.8 11.4 %all_to_all.39 = bf16[4,480,128]{2,1,0:T(8,128)(2,1)S(1)} all-to-all(bf16[4,480,128]{2,1,0:T(8,128)(2,1)S(1)} %broadcast_in_dim.86), channel_id=1, replica_groups=mesh['x'=4,'zh'=2,'zq'=2,'zn'=4,'y'=4,'core'=2] {'y'}, dimensions={0} | all-to-all | bytes 983040 | tf_op jit(solution)/shard_map/all_to_all | solution.py:43
  125.2 2.5 %all_gather.3 = bf16[8,480,128]{2,1,0:T(8,128)(2,1)S(1)} all-gather(bf16[4,480,128]{2,1,0:T(8,128)(2,1)S(1)} %all_to_all.39), channel_id=1, replica_groups=mesh['x'=4,'zh'=2,'zq'=2,'zn'=4,'y'=4,'core'=2] {'core'}, dimensions={0}, use_global_device_ids=true | all-gather | bytes 1474560 | tf_op jit(solution)/shard_map/all_gather | solution.py:127
  127.7 0.0 copy-done.5
  127.7 0.9 convolution_convert_fusion.1
  128.7 22.0 %all_to_all.40 = bf16[4,120,768]{2,1,0:T(8,128)(2,1)S(1)} all-to-all(bf16[4,120,768]{2,1,0:T(8,128)(2,1)S(1)} %bitcast.47), channel_id=1, replica_groups=mesh['x'=4,'zh'=2,'zq'=2,'zn'=4,'y'=4,'core'=2] {'zn'}, dimensions={0} | all-to-all | bytes 1474560 | tf_op jit(solution)/shard_map/all_to_all | solution.py:48
  150.7 0.1 reduce_sum.127
  150.8 0.3 convolution_convert_fusion.2
  151.1 0.1 reshape.286
  151.2 33.3 %all_to_all.41 = bf16[64,4,768]{2,1,0:T(4,128)(2,1)S(1)} all-to-all(bf16[64,4,768]{2,1,0:T(4,128)(2,1)S(1)} %reshape.286), channel_id=1, replica_groups=mesh['x'=4,'zh'=2,'zq'=2,'zn'=4,'y'=4,'core'=2] {'x','zh','zq','zn'}, dimensions={0} | all-to-all | bytes 786432 | tf_op jit(solution)/shard_map/all_to_all | solution.py:137
  184.5 0.1 reshape.289
  184.6 0.1 reduce_sum.128
  184.6 1.0 fusion.4
  (4 shorter events, 0.1 us)
Async XLA Ops:
  0.0 91.5 %copy-start = (bf16[768,1024]{1,0:T(8,128)(2,1)S(1)}, bf16[768,1024]{1,0:T(8,128)(2,1)}, u32[]{:S(2)}) copy-start(bf16[768,1024]{1,0:T(8,128)(2,1)} %param.18) | copy-start | bytes 4718596
  0.0 5.9 %copy-start.1 = (bf16[32,128,128]{2,1,0:T(8,128)(2,1)S(1)}, bf16[32,128,128]{2,1,0:T(8,128)(2,1)}, u32[]{:S(2)}) copy-start(bf16[32,128,128]{2,1,0:T(8,128)(2,1)} %param.13) | copy-start | bytes 3145732
  0.0 6.5 %copy-start.2 = (bf16[32,768]{1,0:T(8,128)(2,1)S(1)}, bf16[32,768]{1,0:T(8,128)(2,1)}, u32[]{:S(2)}) copy-start(bf16[32,768]{1,0:T(8,128)(2,1)} %param.10) | copy-start | bytes 147460
  0.0 19.9 %copy-start.3 = (s32[32,2]{0,1:T(2,128)S(1)}, s32[32,2]{0,1:T(2,128)}, u32[]{:S(2)}) copy-start(s32[32,2]{0,1:T(2,128)} %param.16) | copy-start | bytes 772
  0.0 19.9 %copy-start.4 = (f32[32,2]{0,1:T(2,128)S(1)}, f32[32,2]{0,1:T(2,128)}, u32[]{:S(2)}) copy-start(f32[32,2]{0,1:T(2,128)} %param.17) | copy-start | bytes 772
  113.8 14.0 %copy-start.5 = (bf16[1024,768]{1,0:T(8,128)(2,1)S(1)}, bf16[1024,768]{1,0:T(8,128)(2,1)}, u32[]{:S(2)}) copy-start(bf16[1024,768]{1,0:T(8,128)(2,1)} %param.19) | copy-start | bytes 4718596
